TPU v7x, 256 devices: a whole 4x4x8 slice. The times are simulated.
256 devices in a mesh: row: 32 (over z, x_lo, core), col: 8 (over y, x_hi).
Axes of the slice: x: 4 (x_hi: 2, x_lo: 2; x = x_hi * 2 + x_lo), y: 4, z: 8, core: 2. Of those that a mesh axis runs over, the one named last changes fastest.
Arguments:
- first_homolog_embedding: bfloat16 [128, 1024, 32], P(None, ('row', 'col')), may hold values from -12 to 12
- second_homolog_embedding: bfloat16 [128, 1024, 32], P(None, ('row', 'col')), may hold values from -12 to 12
- token_chain_index: int32 [1024], replicated, may hold values from 0 to 7, never falling along the last dimension, each value on 1 to 384 neighbouring positions
- incoming_pair_state: bfloat16 [1024, 1024, 128], P('row', 'col'), may hold values from -6 to 6
- tensor_mixing_matrix: bfloat16 [1024, 128], replicated, may hold values from -0.1875 to 0.1875
- outer_product_bias: float32 [128], replicated, may hold values from -3 to 3
- transition_norm_gain: float32 [128], replicated, may hold values from 0.5 to 1.5
- transition_gate_weight: bfloat16 [128, 512], replicated, may hold values from -0.5 to 0.5
- transition_up_weight: bfloat16 [128, 512], replicated, may hold values from -0.5 to 0.5
- transition_down_weight: bfloat16 [512, 128], replicated, may hold values from -0.25 to 0.25
- distogram_weight: bfloat16 [128, 64], replicated, may hold values from -0.5 to 0.5
- distogram_bias: float32 [64], replicated, may hold values from -3 to 3
Outputs:
- pair_out: bfloat16 [1024, 1024, 128], P('row', 'col')
- logits: float32 [64, 1024, 1024], P(None, 'row', 'col')
Inputs may be any that keep to these rules, and one draw needn't show every extreme that they name: `token_chain_index`: chain numbers never fall along the tokens; each chain has 1 to 384 tokens and one chain has exactly 384.
All inputs are finite; a program needn't handle non-finite values.
Results may differ from a plain program's by a relative error of at most 0.006.
Values may be sent and summed in bfloat16 or wider, within the bound.
No kernel may reach another device: no remote copies, remote signals or barrier semaphores. Data moves between devices by JAX's collectives and lax.ppermute only.
A program may use at most 64 MiB of HBM per device.

v0:
```python
import jax
import jax.numpy as jnp
from jax import lax
from jax.sharding import PartitionSpec as P


def layer_norm(values, transition_norm_gain):
    center = jnp.mean(values, axis=-1, keepdims=True)
    shifted = values - center
    spread = jnp.mean(shifted * shifted, axis=-1, keepdims=True)
    return shifted * lax.rsqrt(spread + 1e-05) * transition_norm_gain


def transition_rows(
    mid_rows,
    transition_norm_gain,
    transition_gate_weight,
    transition_up_weight,
    transition_down_weight,
):
    mid_float = mid_rows.astype(jnp.float32)
    normed = layer_norm(mid_float, transition_norm_gain).astype(jnp.bfloat16)
    gate_pre = jnp.dot(normed, transition_gate_weight, preferred_element_type=jnp.float32)
    up_pre = jnp.dot(normed, transition_up_weight, preferred_element_type=jnp.float32)
    hidden = (jax.nn.silu(gate_pre) * up_pre).astype(jnp.bfloat16)
    result = mid_float + jnp.dot(hidden, transition_down_weight, preferred_element_type=jnp.float32)
    return result.astype(jnp.bfloat16)


def transition_tile(
    mid_tile,
    transition_norm_gain,
    transition_gate_weight,
    transition_up_weight,
    transition_down_weight,
):
    tile_shape = mid_tile.shape
    rows_all = tile_shape[0] * tile_shape[1]
    grid_piece = min(512, rows_all)
    blocks = mid_tile.reshape(rows_all // grid_piece, grid_piece, tile_shape[2])

    def one_block(rows):
        return transition_rows(
            rows,
            transition_norm_gain,
            transition_gate_weight,
            transition_up_weight,
            transition_down_weight,
        )

    return lax.map(one_block, blocks).reshape(tile_shape)


def mirror_tile(pair_tile):
    row_count = lax.axis_size("row")
    col_count = lax.axis_size("col")
    rows_tile, cols_tile, channels = pair_tile.shape
    row_groups = row_count // col_count
    step_two = lax.all_to_all(
        lax.all_to_all(pair_tile, "col", split_axis=0, concat_axis=1, tiled=True),
        "row",
        split_axis=1,
        concat_axis=0,
        tiled=True,
    )
    regrouped = step_two.reshape(col_count, row_groups, rows_tile // col_count, rows_tile, channels)
    step_three = lax.all_to_all(regrouped, "col", split_axis=0, concat_axis=2, tiled=True)
    return step_three.reshape(cols_tile, rows_tile, channels)


def per_device(
    first_homolog_embedding,
    second_homolog_embedding,
    token_chain_index,
    incoming_pair_state,
    tensor_mixing_matrix,
    outer_product_bias,
    transition_norm_gain,
    transition_gate_weight,
    transition_up_weight,
    transition_down_weight,
    distogram_weight,
    distogram_bias,
):
    row_at = lax.axis_index("row")
    col_at = lax.axis_index("col")
    rows_tile, cols_tile, channels = incoming_pair_state.shape
    sequence_total_count = first_homolog_embedding.shape[0]
    alignment_slab_length = sequence_total_count // 2
    projection_width = first_homolog_embedding.shape[2]
    left_sequence_rows = lax.all_gather(first_homolog_embedding, "col", axis=1, tiled=True)
    pieces = []
    for alignment_slab_index in range(2):
        gathered = lax.all_gather(
            second_homolog_embedding[
                alignment_slab_index
                * alignment_slab_length : (alignment_slab_index + 1)
                * alignment_slab_length
            ],
            ("row", "col"),
            axis=1,
            tiled=True,
        )
        pieces.append(lax.dynamic_slice_in_dim(gathered, col_at * cols_tile, cols_tile, 1))
    right_cols = jnp.concatenate(pieces, 0)
    chain_rows = lax.dynamic_slice_in_dim(token_chain_index, row_at * rows_tile, rows_tile, 0)
    chain_cols = lax.dynamic_slice_in_dim(token_chain_index, col_at * cols_tile, cols_tile, 0)
    same_chain = (chain_rows[:, None] == chain_cols[None, :]).astype(jnp.float32)
    block_rows = max(1, min(rows_tile, 512 // cols_tile))
    block_count = rows_tile // block_rows
    paired_right = right_cols[:alignment_slab_length]
    unpaired_right = right_cols[alignment_slab_length:]

    def outer_block(block_index):
        row_start = block_index * block_rows
        left_block = lax.dynamic_slice_in_dim(left_sequence_rows, row_start, block_rows, 1)
        chain_mask = lax.dynamic_slice_in_dim(same_chain, row_start, block_rows, 0)
        paired_sum = jnp.einsum(
            "sic,sjd->ijcd",
            left_block[:alignment_slab_length],
            paired_right,
            preferred_element_type=jnp.float32,
        )

        def unpaired_terms():
            return jnp.einsum(
                "sic,sjd->ijcd",
                left_block[alignment_slab_length:],
                unpaired_right,
                preferred_element_type=jnp.float32,
            )

        def no_terms():
            return jnp.zeros_like(paired_sum)

        unpaired_sum = lax.cond(jnp.any(chain_mask > 0.5), unpaired_terms, no_terms)
        weight = chain_mask[:, :, None, None]
        homolog_mean = (paired_sum + weight * unpaired_sum) / (
            alignment_slab_length * (1.0 + weight)
        )
        raveled_matrix = homolog_mean.astype(jnp.bfloat16).reshape(
            block_rows * cols_tile, projection_width * projection_width
        )
        inputs = lax.dynamic_slice_in_dim(incoming_pair_state, row_start, block_rows, 0).reshape(
            block_rows * cols_tile, channels
        )
        middle = jnp.dot(raveled_matrix, tensor_mixing_matrix, preferred_element_type=jnp.float32)
        middle = middle + outer_product_bias + inputs.astype(jnp.float32)
        return middle.astype(jnp.bfloat16).reshape(block_rows, cols_tile, channels)

    pair_mid = lax.map(outer_block, jnp.arange(block_count, dtype=jnp.int32)).reshape(
        rows_tile, cols_tile, channels
    )
    pair_out = transition_tile(
        pair_mid,
        transition_norm_gain,
        transition_gate_weight,
        transition_up_weight,
        transition_down_weight,
    )
    mirror_out = mirror_tile(pair_out)
    own_bins = jnp.einsum(
        "ije,ek->kij", pair_out, distogram_weight, preferred_element_type=jnp.float32
    ).astype(jnp.bfloat16)
    other_bins = jnp.einsum(
        "jie,ek->kij", mirror_out, distogram_weight, preferred_element_type=jnp.float32
    ).astype(jnp.bfloat16)
    logits = (
        own_bins.astype(jnp.float32)
        + other_bins.astype(jnp.float32)
        + distogram_bias[:, None, None]
    )
    return (pair_out, logits)


def solution(mesh):
    placed = (
        P(None, ("row", "col"), None),
        P(None, ("row", "col"), None),
        P(),
        P("row", "col", None),
        P(),
        P(),
        P(),
        P(),
        P(),
        P(),
        P(),
        P(),
    )
    return jax.shard_map(
        per_device,
        mesh=mesh,
        in_specs=placed,
        out_specs=(P("row", "col", None), P(None, "row", "col")),
        check_vma=False,
    )
```

profile of v0, /device:TPU:2, one launch (start us, length us, event | category | flops | bytes accessed | tf_op | source)
XLA Modules:
  0.0 1669.1 jit_solution(15646083899122393495)
XLA Ops:
  7.2 1.5 fusion.57
  11.1 35.4 %all_gather.9 = bf16[128,32,32]{0,2,1:T(8,128)(2,1)S(1)} all-gather(bf16[128,4,32]{0,2,1:T(8,128)(2,1)} %param.18), channel_id=1, replica_groups=mesh['row'=32,'col'=8] {'col'}, dimensions={1}, use_global_device_ids=true | all-gather | bytes 294912 | tf_op jit(solution)/shard_map/all_gather | solution.py:91
  46.6 686.4 %all-gather.3.cloned.1.call-done = bf16[64,1024,32]{0,2,1:T(8,128)(2,1)} async-done(((bf16[64,4,32]{0,2,1:T(8,128)(2,1)}), bf16[64,1024,32]{0,2,1:T(8,128)(2,1)}) %all-gather.3.cloned.1.call-update) | async-done | bytes 4194320 | tf_op jit(solution)/shard_map/all_gather | solution.py:94
  733.0 1.3 constant_dynamic-slice_fusion.4
  735.4 720.9 %all-gather.5.cloned.1.call-done = bf16[64,1024,32]{0,2,1:T(8,128)(2,1)} async-done(((bf16[64,4,32]{0,2,1:T(8,128)(2,1)}), bf16[64,1024,32]{0,2,1:T(8,128)(2,1)}) %all-gather.5.cloned.1.call-update) | async-done | bytes 4194320 | tf_op jit(solution)/shard_map/all_gather | solution.py:94
  1456.3 1.3 constant_dynamic-slice_fusion.3
  1459.3 72.8 %while.20 = (s32[]{:T(128)}, bf16[8,4,128,128]{3,2,1,0:T(8,128)(2,1)}, s32[8]{0:T(128)}, bf16[128,32,32]{0,2,1:T(8,128)(2,1)S(1)}, bf16[64,128,32]{1,0,2:T(8,128...) while((s32[]{:T(128)}, ...), condition=%wide.region_4.5_spmd, body=%wide.region_0.4_spmd.sunk | while | flops 270796800 | bytes 16014713 | solution.py:151
  1459.3 1.3 dynamic_slice.59
  1532.1 46.6 %while.21 = (s32[]{:T(128)}, bf16[8,512,128]{2,1,0:T(8,128)(2,1)}, bf16[8,512,128]{2,1,0:T(8,128)(2,1)}, f32[128]{0:T(128)}, bf16[128,512]{1,0:T(8,128)(2,1)S(1)...) while((s32[]{:T(128)}, bf16[8,512,128]{2,1,0:T(8,128)(2,1)}, ...), condition=%wide.region_8.9_spmd, body=%wide.region_5.8_spmd.sunk | while | flops 204145152 | bytes 3301981 | solution.py:51
  1534.3 1.3 fusion.88
  1535.5 2.4 fusion.89
  1541.4 2.4 fusion.89
  1545.9 1.3 fusion.88
  1547.2 2.4 fusion.89
  1553.0 2.4 fusion.89
  1558.9 2.4 fusion.89
  1563.4 1.3 fusion.88
  1564.7 2.4 fusion.89
  1570.5 2.4 fusion.89
  1576.4 2.4 fusion.89
  1578.7 20.7 %all_to_all.48 = bf16[32,128,128]{2,1,0:T(8,128)(2,1)S(1)} all-to-all(bf16[32,128,128]{2,1,0:T(8,128)(2,1)} %bitcast.126), channel_id=1, replica_groups=mesh['row'=32,'col'=8] {'col'}, dimensions={0} | all-to-all | bytes 2097152 | tf_op jit(solution)/shard_map/all_to_all | solution.py:60
  1600.3 38.7 %all_to_all.49 = bf16[4,1024,128]{2,0,1:T(4,128)(2,1)S(1)} all-to-all(bf16[4,1024,128]{2,0,1:T(4,128)(2,1)S(1)} %copy.46), channel_id=1, replica_groups=mesh['row'=32,'col'=8] {'row'}, dimensions={1} | all-to-all | bytes 2097152 | tf_op jit(solution)/shard_map/all_to_all | solution.py:59
  1639.3 19.6 %all_to_all.50 = bf16[8,4,4,32,128]{4,3,2,1,0:T(8,128)(2,1)S(1)} all-to-all(bf16[8,4,4,32,128]{4,3,2,1,0:T(8,128)(2,1)S(1)} %bitcast.131), channel_id=1, replica_groups=mesh['row'=32,'col'=8] {'col'}, dimensions={0} | all-to-all | bytes 2097152 | tf_op jit(solution)/shard_map/all_to_all | solution.py:67
  1660.7 1.6 copy.50
  (239 shorter events, 98.3 us)
Async XLA Ops:
  7.2 1652.4 %copy-start = (bf16[128,64]{0,1:T(8,128)(2,1)S(1)}, bf16[128,64]{0,1:T(8,128)(2,1)}, u32[]{:S(2)}) copy-start(bf16[128,64]{0,1:T(8,128)(2,1)} %param.28) | copy-start | bytes 49156
  7.2 725.8 %all-gather.3.cloned.1.call-start = ((), (), s32[]{:S(2)}) async-start(), calls=%async_computation.3 | async-start | bytes 8421376 | tf_op jit(solution)/shard_map/all_gather | solution.py:94
  8.8 1447.5 %all-gather.5.cloned.1.call-start = ((), (), s32[]{:S(2)}) async-start(), calls=%async_computation.4 | async-start | bytes 8421376 | tf_op jit(solution)/shard_map/all_gather | solution.py:94
  1459.3 72.8 %copy-start.2 = (bf16[128,512]{1,0:T(8,128)(2,1)S(1)}, bf16[128,512]{1,0:T(8,128)(2,1)}, u32[]{:S(2)}) copy-start(bf16[128,512]{1,0:T(8,128)(2,1)} %param.25) | copy-start | bytes 393220
  1459.3 4.3 copy-start.4
  1465.4 1.8 copy-start.7
  1465.5 2.9 copy-start.5
  1468.4 4.3 copy-start.4
  1474.5 1.8 copy-start.7
  1474.6 2.9 copy-start.5
  1477.5 4.3 copy-start.4
  1483.6 1.8 copy-start.7
  1483.7 2.9 copy-start.5
  1486.6 4.3 copy-start.4
  1492.7 1.8 copy-start.7
  1492.8 2.9 copy-start.5
  1495.7 4.3 copy-start.4
  1501.8 2.9 copy-start.5
  1504.8 4.3 copy-start.4
  1510.9 2.9 copy-start.5
  1513.9 4.3 copy-start.4
  1520.0 2.9 copy-start.5
  1523.0 4.3 copy-start.4
  1529.1 2.9 copy-start.5
  (22 other events, 28.4 us)
Sparse Core Ops, SparseCore 0:
  9.9 723.0 all-gather.2
  734.8 721.4 all-gather.4
where the time goes:
time: 1670 us
  waiting for transfers between devices  1410 us (84%)
  blocking collectives  114 us (7%)
  local copies, waits for them, and re-layouts  47.7 us (3%)
  matrix products  46.7 us (3%)
  other arithmetic  27.3 us (2%)
    all_gather x2, waiting for transfers between devices, per_device(): lax.all_gather(second_homolog_embedding[alignment_slab_index * alignment_...  1410 us
    all_to_all x1, blocking collectives, mirror_tile(): lax.all_to_all(lax.all_to_all(pair_tile, 'col', split_axis=0, concat_axis...  38.7 us
    all_gather x1, blocking collectives, per_device(): lax.all_gather(first_homolog_embedding, 'col', axis=1, tiled=True)  35.4 us
  transfers between devices with their start and end apart: 2, of which 2 were waited for; matrix products, arithmetic and copies ran while one was open for 0% of the time, Pallas kernels for 0%

commit v1 on v0

--- a/solution.py
+++ b/solution.py
@@ -91,16 +91,15 @@
     left_sequence_rows = lax.all_gather(first_homolog_embedding, "col", axis=1, tiled=True)
     pieces = []
     for alignment_slab_index in range(2):
-        gathered = lax.all_gather(
-            second_homolog_embedding[
-                alignment_slab_index
-                * alignment_slab_length : (alignment_slab_index + 1)
-                * alignment_slab_length
-            ],
-            ("row", "col"),
-            axis=1,
-            tiled=True,
-        )
+        x = second_homolog_embedding[
+            alignment_slab_index
+            * alignment_slab_length : (alignment_slab_index + 1)
+            * alignment_slab_length
+        ]
+        size = lax.axis_size(("row", "col"))
+        parts = jnp.stack([x for _ in range(size)])
+        parts = lax.all_to_all(parts, ("row", "col"), split_axis=0, concat_axis=0)
+        gathered = jnp.concatenate(parts, axis=1)
         pieces.append(lax.dynamic_slice_in_dim(gathered, col_at * cols_tile, cols_tile, 1))
     right_cols = jnp.concatenate(pieces, 0)
     chain_rows = lax.dynamic_slice_in_dim(token_chain_index, row_at * rows_tile, rows_tile, 0)

time: 1670 us -> 446 us (0.27)
  waiting for transfers between devices: 1410 us -> 117 us
  local copies, waits for them, and re-layouts: 47.7 us -> 104 us
  starting transfers between devices: 0.08 us -> 24.5 us
    all_gather x2 -> x0, waiting for transfers between devices: 1410 us -> none  [per_device(): lax.all_gather(second_homolog_embedding[alignment_slab_index * alignment_...]
    all_to_all x0 -> x2, waiting for transfers between devices: none -> 117 us  [per_device(): parts = lax.all_to_all(parts, ('row', 'col'), split_axis=0, concat_axis=0)]
    unnamed x9 -> x25, local copies, waits for them, and re-layouts: 1.79 us -> 68.6 us
    all_to_all x0 -> x2, starting transfers between devices: none -> 24.5 us  [per_device(): parts = lax.all_to_all(parts, ('row', 'col'), split_axis=0, concat_axis=0)]
  transfers between devices with their start and end apart: 2 -> 2, of which waited for: 2 -> 2; matrix products, arithmetic and copies ran while one was open for 0% -> 8% of each run, Pallas kernels for 0% -> 0%
where the time goes in v1:
time: 446 us; the launch traced here: 443 us
  waiting for transfers between devices  117 us (26%)
  blocking collectives  115 us (26%)
  local copies, waits for them, and re-layouts  104 us (23%)
  matrix products  48.7 us (11%)
  starting transfers between devices  24.5 us (5%)
  other arithmetic  22.9 us (5%)
  loops' own time  10.9 us (2%)
    all_to_all x2, waiting for transfers between devices, per_device(): parts = lax.all_to_all(parts, ('row', 'col'), split_axis=0, concat_axis=0)  117 us
    unnamed x25, local copies, waits for them, and re-layouts  68.6 us
    all_gather x1, blocking collectives, per_device(): lax.all_gather(first_homolog_embedding, 'col', axis=1, tiled=True)  40.2 us
    all_to_all x1, blocking collectives, mirror_tile(): lax.all_to_all(lax.all_to_all(pair_tile, 'col', split_axis=0, concat_axis...  33.8 us
    all_to_all x2, starting transfers between devices, per_device(): parts = lax.all_to_all(parts, ('row', 'col'), split_axis=0, concat_axis=0)  24.5 us
    all_to_all x1, blocking collectives, mirror_tile(): lax.all_to_all(pair_tile, 'col', split_axis=0, concat_axis=1, tiled=True)  20.7 us
    all_to_all x1, blocking collectives, mirror_tile(): lax.all_to_all(regrouped, 'col', split_axis=0, concat_axis=2, tiled=True)  19.8 us
    dot_general x8, matrix products, transition_rows(): jnp.dot(hidden, transition_down_weight, preferred_element_type=jnp.float32)  18.2 us
  transfers between devices with their start and end apart: 2, of which 2 were waited for; matrix products, arithmetic and copies ran while one was open for 8% of the time, Pallas kernels for 0%

profile of v1, /device:TPU:2, one launch (start us, length us, event | category | flops | bytes accessed | tf_op | source)
XLA Modules:
  0.0 443.0 jit_solution(4505741472401098194)
XLA Ops:
  1.6 5.3 %broadcast_bitcast_fusion.1 = bf16[256,4,32,64]{3,2,1,0:T(8,128)(2,1)} fusion(bf16[64,4,32]{0,2,1:T(8,128)(2,1)S(1)} %get-tuple-element.190), kind=kLoop, calls=%fused_computation.71 | loop fusion | bytes 4210688
  6.9 14.0 %reshape.76 = bf16[256,2,4096]{2,1,0:T(2,128)(2,1)} reshape(bf16[256,4,32,64]{3,2,1,0:T(8,128)(2,1)} %broadcast_bitcast_fusion.1) | data formatting | bytes 8388608
  20.9 15.7 %all-to-all-start = ((bf16[256,2,4096]{2,1,0:T(2,128)(2,1)}), bf16[256,2,4096]{2,1,0:T(2,128)(2,1)}, u32[]{:S(2)}, u32[]{:S(2)}) async-start(bf16[256,2,4096]{2,1,0:T(2,128)(2,1)} %reshape.76), calls=%async_computation | async-start | bytes 8388608 | tf_op jit(solution)/shard_map/all_to_all | solution.py:101
  36.6 5.3 %broadcast_bitcast_fusion = bf16[256,4,32,64]{3,2,1,0:T(8,128)(2,1)} fusion(bf16[64,4,32]{0,2,1:T(8,128)(2,1)S(1)} %get-tuple-element.189), kind=kLoop, calls=%fused_computation.70 | loop fusion | bytes 4210688
  41.9 14.0 %reshape.78 = bf16[256,2,4096]{2,1,0:T(2,128)(2,1)} reshape(bf16[256,4,32,64]{3,2,1,0:T(8,128)(2,1)} %broadcast_bitcast_fusion) | data formatting | bytes 8388608
  55.9 76.9 %all-to-all-done = bf16[256,2,4096]{2,1,0:T(2,128)(2,1)} async-done(((bf16[256,2,4096]{2,1,0:T(2,128)(2,1)}), bf16[256,2,4096]{2,1,0:T(2,128)(2,1)}, u32[]{:S(2)}, u32[]{:S(2)}) %all-to-all-start) | async-done | bytes 4194336 | tf_op jit(solution)/shard_map/all_to_all | solution.py:101
  132.7 8.8 %all-to-all-start.1 = ((bf16[256,2,4096]{2,1,0:T(2,128)(2,1)}), bf16[256,2,4096]{2,1,0:T(2,128)(2,1)}, u32[]{:S(2)}, u32[]{:S(2)}) async-start(bf16[256,2,4096]{2,1,0:T(2,128)(2,1)} %reshape.78), calls=%async_computation.1 | async-start | bytes 8388608 | tf_op jit(solution)/shard_map/all_to_all | solution.py:101
  143.1 40.2 %all_gather.3 = bf16[128,32,32]{0,2,1:T(8,128)(2,1)S(1)} all-gather(bf16[128,4,32]{0,2,1:T(8,128)(2,1)S(1)} %copy-done.3), channel_id=1, replica_groups=mesh['row'=32,'col'=8] {'col'}, dimensions={1}, use_global_device_ids=true | all-gather | bytes 294912 | tf_op jit(solution)/shard_map/all_gather | solution.py:91
  183.4 14.2 %reshape.77 = bf16[256,4,32,64]{3,2,1,0:T(8,128)(2,1)} reshape(bf16[256,2,4096]{2,1,0:T(2,128)(2,1)} %all-to-all-done) | data formatting | bytes 8388608
  197.7 40.1 %all-to-all-done.1 = bf16[256,2,4096]{2,1,0:T(2,128)(2,1)} async-done(((bf16[256,2,4096]{2,1,0:T(2,128)(2,1)}), bf16[256,2,4096]{2,1,0:T(2,128)(2,1)}, u32[]{:S(2)}, u32[]{:S(2)}) %all-to-all-start.1) | async-done | bytes 4194336 | tf_op jit(solution)/shard_map/all_to_all | solution.py:101
  237.7 14.2 %reshape.79 = bf16[256,4,32,64]{3,2,1,0:T(8,128)(2,1)} reshape(bf16[256,2,4096]{2,1,0:T(2,128)(2,1)} %all-to-all-done.1) | data formatting | bytes 8388608
  256.9 61.6 %while.20 = (s32[]{:T(128)}, bf16[8,4,128,128]{3,2,1,0:T(8,128)(2,1)}, s32[8]{0:T(128)S(1)}, bf16[128,32,32]{0,2,1:T(8,128)(2,1)S(1)}, bf16[64,128,32]{1,0,2:T(8...) while((s32[]{:T(128)}, ...), condition=%wide.region_4.5_spmd, body=%wide.region_0.4_spmd.sunk | while | flops 270796800 | bytes 14824685 | solution.py:150
  318.5 45.8 %while.21 = (s32[]{:T(128)}, bf16[8,512,128]{2,1,0:T(8,128)(2,1)}, bf16[8,512,128]{2,1,0:T(8,128)(2,1)}, f32[128]{0:T(128)S(1)}, bf16[128,512]{1,0:T(8,128)(2,1)...) while((s32[]{:T(128)}, bf16[8,512,128]{2,1,0:T(8,128)(2,1)}, ...), condition=%wide.region_8.9_spmd, body=%wide.region_5.8_spmd.sunk | while | flops 204145152 | bytes 3301981 | solution.py:51
  322.0 2.3 fusion.89
  327.7 2.3 fusion.89
  333.4 2.3 fusion.89
  339.1 2.3 fusion.89
  344.8 2.3 fusion.89
  350.5 2.3 fusion.89
  356.3 2.3 fusion.89
  362.0 2.3 fusion.89
  364.3 20.7 %all_to_all.58 = bf16[32,128,128]{2,1,0:T(8,128)(2,1)S(1)} all-to-all(bf16[32,128,128]{2,1,0:T(8,128)(2,1)} %bitcast.140), channel_id=1, replica_groups=mesh['row'=32,'col'=8] {'col'}, dimensions={0} | all-to-all | bytes 2097152 | tf_op jit(solution)/shard_map/all_to_all | solution.py:60
  385.9 33.8 %all_to_all.59 = bf16[4,1024,128]{2,0,1:T(4,128)(2,1)S(1)} all-to-all(bf16[4,1024,128]{2,0,1:T(4,128)(2,1)S(1)} %copy.46), channel_id=1, replica_groups=mesh['row'=32,'col'=8] {'row'}, dimensions={1} | all-to-all | bytes 2097152 | tf_op jit(solution)/shard_map/all_to_all | solution.py:59
  420.1 19.8 %all_to_all.60 = bf16[8,4,4,32,128]{4,3,2,1,0:T(8,128)(2,1)S(1)} all-to-all(bf16[8,4,4,32,128]{4,3,2,1,0:T(8,128)(2,1)S(1)} %bitcast.145), channel_id=1, replica_groups=mesh['row'=32,'col'=8] {'col'}, dimensions={0} | all-to-all | bytes 2097152 | tf_op jit(solution)/shard_map/all_to_all | solution.py:67
  (172 shorter events, 95.6 us)
Async XLA Ops:
  0.6 439.8 %copy-start = (bf16[128,64]{0,1:T(8,128)(2,1)S(1)}, bf16[128,64]{0,1:T(8,128)(2,1)}, u32[]{:S(2)}) copy-start(bf16[128,64]{0,1:T(8,128)(2,1)} %param.28) | copy-start | bytes 49156
  20.9 111.9 %all-to-all-start = ((bf16[256,2,4096]{2,1,0:T(2,128)(2,1)}), bf16[256,2,4096]{2,1,0:T(2,128)(2,1)}, u32[]{:S(2)}, u32[]{:S(2)}) async-start(bf16[256,2,4096]{2,1,0:T(2,128)(2,1)} %reshape.76), calls=%async_computation | async-start | bytes 8388608 | tf_op jit(solution)/shard_map/all_to_all | solution.py:101
  55.9 87.2 %copy-start.3 = (bf16[128,4,32]{0,2,1:T(8,128)(2,1)S(1)}, bf16[128,4,32]{0,2,1:T(8,128)(2,1)}, u32[]{:S(2)}) copy-start(bf16[128,4,32]{0,2,1:T(8,128)(2,1)} %param.18) | copy-start | bytes 98308
  132.7 105.0 %all-to-all-start.1 = ((bf16[256,2,4096]{2,1,0:T(2,128)(2,1)}), bf16[256,2,4096]{2,1,0:T(2,128)(2,1)}, u32[]{:S(2)}, u32[]{:S(2)}) async-start(bf16[256,2,4096]{2,1,0:T(2,128)(2,1)} %reshape.78), calls=%async_computation.1 | async-start | bytes 8388608 | tf_op jit(solution)/shard_map/all_to_all | solution.py:101
  251.9 4.9 %copy-start.6 = (bf16[1024,128]{1,0:T(8,128)(2,1)S(1)}, bf16[1024,128]{1,0:T(8,128)(2,1)}, u32[]{:S(2)}) copy-start(bf16[1024,128]{1,0:T(8,128)(2,1)} %param.22) | copy-start | bytes 786436
  251.9 5.0 %copy-start.8 = (f32[128]{0:T(128)S(1)}, f32[128]{0:T(128)}, u32[]{:S(2)}) copy-start(f32[128]{0:T(128)} %param.23) | copy-start | bytes 1540
  256.9 61.6 %copy-start.2 = (bf16[128,512]{1,0:T(8,128)(2,1)S(1)}, bf16[128,512]{1,0:T(8,128)(2,1)}, u32[]{:S(2)}) copy-start(bf16[128,512]{1,0:T(8,128)(2,1)} %param.25) | copy-start | bytes 393220
  256.9 61.6 %copy-start.4 = (f32[128]{0:T(128)S(1)}, f32[128]{0:T(128)}, u32[]{:S(2)}) copy-start(f32[128]{0:T(128)} %param.24) | copy-start | bytes 1540
  256.9 61.6 %copy-start.7 = (bf16[128,512]{1,0:T(8,128)(2,1)S(1)}, bf16[128,512]{1,0:T(8,128)(2,1)}, u32[]{:S(2)}) copy-start(bf16[128,512]{1,0:T(8,128)(2,1)} %param.26) | copy-start | bytes 393220
  419.9 21.0 %copy-start.1 = (bf16[8,512,128]{2,1,0:T(8,128)(2,1)S(1)}, bf16[8,512,128]{2,1,0:T(8,128)(2,1)}, u32[]{:S(2)}) copy-start(bf16[8,512,128]{2,1,0:T(8,128)(2,1)} %get-tuple-element.101) | copy-start | bytes 3145732
  419.9 21.0 %copy-start.5 = (f32[64]{0:T(128)S(1)}, f32[64]{0:T(128)}, u32[]{:S(2)}) copy-start(f32[64]{0:T(128)} %param.29) | copy-start | bytes 772
